TPU v7x, 256 devices: a whole 4x4x8 slice. The times are simulated.
256 devices in a mesh: row: 8 (over z), col: 32 (over x, y, core).
Axes of the slice: x: 4, y: 4, z: 8, core: 2. Of those that a mesh axis runs over, the one named last changes fastest.
Arguments:
- h_values: float32 [8, 512, 4096], P('row', 'col'), as said below
- h_places: int32 [8, 512], P('row', 'col'), may hold values from 0 to 15, as said below
- h_counts: int32 [8, 32], P('row', 'col'), may hold values from 0 to 16, as said below
- p_values: float32 [8, 512, 4096], P('row', 'col'), as said below
- p_places: int32 [8, 512], P('row', 'col'), may hold values from 0 to 15, as said below
- p_counts: int32 [8, 32], P('row', 'col'), may hold values from 0 to 16, as said below
- s_values: float32 [8, 512, 4096], P('row', 'col'), as said below
- s_places: int32 [8, 512], P('row', 'col'), may hold values from 0 to 15, as said below
- s_counts: int32 [8, 32], P('row', 'col'), may hold values from 0 to 16, as said below
- x_places: int32 [8, 512], P('row', 'col'), may hold values from 0 to 15, as said below
- x_counts: int32 [8, 32], P('row', 'col'), may hold values from 0 to 16, as said below
Outputs:
- gradient: float32 [8, 512, 4096], P('row', 'col')
Inputs may be any that keep to these rules, and one draw needn't show every extreme that they name: `h_places`: in each tile the 16 entries are a permutation of the tile's positions; the first count entries are the present blocks. Every pattern is symmetric, holds every block whose block row and block column lie in the same row panel, and every block (i, j) whose cyclic block distance min(|i - j|, 64 - |i - j|) is 2 or less or exactly 32. `p_places`: as for h_places. `s_places`: as for h_places. `x_places`: as for h_places. `h_counts`: every tile whose block columns lie in its own row panel is full. `p_counts`: as for h_counts. `s_counts`: as for h_counts. `x_counts`: as for h_counts. `h_values`: the assembled H is symmetric. `p_values`: the assembled P is symmetric. `s_values`: the assembled S is symmetric.
All inputs are finite; a program needn't handle non-finite values.
Results may differ from a plain program's by a relative error of at most 0.000088.
Values sent between devices are 32-bit elements; how exact they have to be, the bound alone decides.
A program may use at most 64 MiB of HBM per device.

v0:
```python
import jax
import jax.numpy as jnp
from jax import lax
from jax.sharding import PartitionSpec as P

BS = 64
TC = 2


def from_root(value, axis, source):
    kept = jnp.where(lax.axis_index(axis) == source, value, 0).astype(value.dtype)
    return lax.psum(kept, axis)


def assemble(values, places, counts):
    blocks_in = values[0]
    capacity = blocks_in.shape[0]
    slot_ids = lax.iota(jnp.int32, capacity)
    matches = (places[0][:, None] == slot_ids[None, :]) & (slot_ids[:, None] < counts[0, 0])
    spread = jnp.dot(matches.astype(jnp.float32).T, blocks_in, precision=lax.Precision.HIGHEST)
    row_count = capacity // TC
    return (
        spread.reshape(row_count, TC, BS, BS).transpose(0, 2, 1, 3).reshape(row_count * BS, TC * BS)
    )


def expand_mask(present, row_count, col_count):
    flags = present.reshape(row_count, col_count)
    return jnp.broadcast_to(flags[:, None, :, None], (row_count, BS, col_count, BS)).reshape(
        row_count * BS, col_count * BS
    )


def tile_mask(places, counts):
    capacity = places.shape[1]
    slot_ids = lax.iota(jnp.int32, capacity)
    matches = (places[0][:, None] == slot_ids[None, :]) & (slot_ids[:, None] < counts[0, 0])
    present = jnp.sum(matches.astype(jnp.float32), axis=0)
    return expand_mask(present, capacity // TC, TC)


def tile_to_slots(tile, places, counts):
    row_count = tile.shape[0] // BS
    blocks = (
        tile.reshape(row_count, BS, TC, BS).transpose(0, 2, 1, 3).reshape(row_count * TC, BS * BS)
    )
    picked = jnp.take(blocks, places[0], axis=0)
    slot_ids = lax.iota(jnp.int32, places.shape[1])
    used = (slot_ids < counts[0, 0]).astype(jnp.float32)
    return (picked * used[:, None])[None]


def shards(
    h_values,
    h_places,
    h_counts,
    p_values,
    p_places,
    p_counts,
    s_values,
    s_places,
    s_counts,
    x_places,
    x_counts,
):
    col_index = lax.axis_index("col")
    h_tile = assemble(h_values, h_places, h_counts)
    p_tile = assemble(p_values, p_places, p_counts)
    s_tile = assemble(s_values, s_places, s_counts)
    mask_tile = tile_mask(x_places, x_counts)
    row_width = h_tile.shape[0]
    col_width = h_tile.shape[1]
    p_columns, s_columns = (
        lax.all_gather(p_tile, "row", axis=0, tiled=True),
        lax.all_gather(s_tile, "row", axis=0, tiled=True),
    )
    product = jnp.dot(
        lax.all_gather(h_tile, "col", axis=1, tiled=True),
        p_columns,
        precision=lax.Precision.HIGHEST,
    )
    y_tile = mask_tile * product
    y_panel = lax.all_gather(y_tile, "col", axis=1, tiled=True)
    x_tile = mask_tile * jnp.dot(y_panel, s_columns, precision=lax.Precision.HIGHEST)
    per_panel = row_width // col_width
    source_row = col_index // per_panel
    offset = col_index % per_panel * col_width
    y_part = lax.dynamic_slice_in_dim(y_panel, offset, col_width, 0)
    y_mirror = from_root(y_part, "row", source_row)
    far_part = lax.dot_general(
        lax.all_gather(s_tile, "col", axis=1, tiled=True),
        y_mirror,
        (((1,), (1,)), ((), ())),
        precision=lax.Precision.HIGHEST,
    )
    mirrored = mask_tile * far_part
    return tile_to_slots(x_tile + mirrored, x_places, x_counts)


def solution(mesh):
    in_specs = (
        P("row", "col", None),
        P("row", "col"),
        P("row", "col"),
        P("row", "col", None),
        P("row", "col"),
        P("row", "col"),
        P("row", "col", None),
        P("row", "col"),
        P("row", "col"),
        P("row", "col"),
        P("row", "col"),
    )
    out_specs = P("row", "col", None)
    return jax.shard_map(shards, mesh=mesh, in_specs=in_specs, out_specs=out_specs, check_vma=False)
```

profile of v0, /device:TPU:2, one launch (start us, length us, event | category | flops | bytes accessed | tf_op | source)
XLA Modules:
  0.0 405.1 jit_solution(8840308818379448259)
XLA Ops:
  6.5 0.0 all-gather.8.cloned.1.call-start
  7.3 1.1 dot_general.34
  8.4 0.0 copy-start.2
  8.4 1.3 convolution_bitcast_fusion.1
  9.8 0.3 copy.26
  10.0 0.9 reshape.190
  10.9 0.0 all-gather.8.cloned.1.call-update
  10.9 0.0 all-gather.6.cloned.1.call-start
  11.6 0.0 copy-done
  11.6 0.2 dot_general.31
  11.9 0.0 copy-done.2
  11.9 0.7 convolution_bitcast_fusion.2
  12.6 0.3 copy.24
  12.8 0.9 reshape.189
  13.7 0.0 all-gather.6.cloned.1.call-update
  13.7 0.0 all-gather.10.cloned.1.call-start
  14.4 0.0 copy-done.4
  14.4 0.1 convert_reduce_fusion
  14.5 0.1 broadcast_in_dim.19
  14.6 0.2 broadcast_in_dim.20
  14.8 0.3 reshape.188
  15.1 0.0 copy-start.1
  15.2 0.0 copy-start.3
  15.2 40.0 %all-gather.8.cloned.1.call-done = f32[4096,128]{0,1:T(8,128)} async-done(((f32[512,128]{0,1:T(8,128)}), f32[4096,128]{0,1:T(8,128)}) %all-gather.8.cloned.1.call-update) | async-done | bytes 2097168 | tf_op jit(solution)/shard_map/all_gather | solution.py:74
  55.1 59.1 %all-gather.6.cloned.1.call-done = f32[512,4096]{0,1:T(8,128)} async-done(((f32[512,128]{0,1:T(8,128)}), f32[512,4096]{0,1:T(8,128)}) %all-gather.6.cloned.1.call-update) | async-done | bytes 8388624 | tf_op jit(solution)/shard_map/all_gather | solution.py:78
  114.2 16.5 %convolution_multiply_fusion = f32[512,128]{1,0:T(8,128)} fusion(f32[512,128]{1,0:T(8,128)S(1)} %reshape.188, f32[512,4096]{0,1:T(8,128)} %all-gather.6.cloned.1.call-done, f32[4096,128]{0,1:T(8,128)} %all-gather.8.cloned.1.call-done), kind=kOutput, calls=%fused_computation.7 | convolution fusion | flops 3221291008 | bytes 11010048 | tf_op jit(solution)/shard_map/dot_general | solution.py:77
  130.7 0.0 all-gather.10.cloned.1.call-update
  130.8 0.0 all-gather.12.cloned.1.call-start
  131.5 0.2 dot_general.38
  131.7 0.7 convolution_bitcast_fusion
  132.4 0.3 copy.28
  132.7 0.9 reshape.191
  133.5 0.0 all-gather.12.cloned.1.call-update
  133.6 0.0 all-gather.14.cloned.1.call-start
  133.6 0.5 all-gather.14.cloned.1.call-update
  134.2 0.2 all-reduce.2.cloned.1.call-start
  134.4 60.4 %all-gather.10.cloned.1.call-done = f32[512,4096]{1,0:T(8,128)} async-done(((f32[512,128]{1,0:T(8,128)}), f32[512,4096]{1,0:T(8,128)}) %all-gather.10.cloned.1.call-update) | async-done | bytes 8388624 | tf_op jit(solution)/shard_map/all_gather | solution.py:83
  194.8 3.2 dynamic-slice_select_fusion
  198.0 0.0 all-reduce.2.cloned.1.call-update
  198.0 39.7 %all-gather.12.cloned.1.call-done = f32[4096,128]{0,1:T(8,128)} async-done(((f32[512,128]{0,1:T(8,128)}), f32[4096,128]{0,1:T(8,128)}) %all-gather.12.cloned.1.call-update) | async-done | bytes 2097168 | tf_op jit(solution)/shard_map/all_gather | solution.py:75
  237.7 9.3 %fusion.29 = f32[512,128]{1,0:T(8,128)S(1)} fusion(f32[512,4096]{1,0:T(8,128)} %all-gather.10.cloned.1.call-done, f32[4096,128]{0,1:T(8,128)} %all-gather.12.cloned.1.call-done), kind=kOutput, calls=%fused_computation.48 | convolution fusion | flops 3221225472 | bytes 10747904 | tf_op jit(solution)/shard_map/dot_general | solution.py:84
  247.0 49.5 %all-gather.14.cloned.1.call-done = f32[512,4096]{0,1:T(8,128)} async-done(((f32[512,128]{0,1:T(8,128)}), f32[512,4096]{0,1:T(8,128)}) %all-gather.14.cloned.1.call-update) | async-done | bytes 8388624 | tf_op jit(solution)/shard_map/all_gather | solution.py:91
  296.6 83.7 %all-reduce.2.cloned.1.call-done = f32[128,4096]{1,0:T(8,128)} async-done(((f32[128,4096]{1,0:T(8,128)}), f32[128,4096]{1,0:T(8,128)}) %all-reduce.2.cloned.1.call-update) | async-done | bytes 2097168 | tf_op jit(solution)/shard_map/psum | solution.py:12
  380.3 16.0 %fusion = f32[512,128]{1,0:T(8,128)S(1)} fusion(f32[512,128]{1,0:T(8,128)S(1)} %reshape.188, f32[512,128]{1,0:T(8,128)S(1)} %fusion.29, f32[512,4096]{0,1:T(8,128)} %all-gather.14.cloned.1.call-done, f32[128,4096]{1,0:T(8,128)} %all-reduce.2.cloned.1.call-done), kind=kOutput, calls=%fused_computation.6 | convolution fusion | flops 3221356544 | bytes 11272192 | tf_op jit(solution)/shard_map/dot_general | solution.py:90
  396.3 0.3 reshape.192
  396.7 0.2 reshape.193
  396.9 0.6 gather_fusion
  397.5 0.8 fusion.7
  (13 shorter events, 0.1 us)
Async XLA Ops:
  6.5 5.1 %copy-start = (f32[1,16,4096]{2,1,0:T(8,128)S(1)}, f32[1,16,4096]{2,1,0:T(8,128)}, u32[]{:S(2)}) copy-start(f32[1,16,4096]{2,1,0:T(8,128)} %param.11) | copy-start | bytes 786436
  6.5 48.6 %all-gather.8.cloned.1.call-start = ((), (), s32[]{:S(2)}) async-start(), calls=%async_computation.1 | async-start | bytes 2359296 | tf_op jit(solution)/shard_map/all_gather | solution.py:74
  8.4 3.5 copy-start.2
  10.9 3.5 copy-start.4
  10.9 103.3 %all-gather.6.cloned.1.call-start = ((), (), s32[]{:S(2)}) async-start(), calls=%async_computation | async-start | bytes 8650752 | tf_op jit(solution)/shard_map/all_gather | solution.py:78
  13.7 181.1 %all-gather.10.cloned.1.call-start = ((), (), s32[]{:S(2)}) async-start(), calls=%async_computation.2 | async-start | bytes 8650752 | tf_op jit(solution)/shard_map/all_gather | solution.py:83
  15.1 116.3 %copy-start.1 = (f32[1,16,4096]{2,1,0:T(8,128)S(1)}, f32[1,16,4096]{2,1,0:T(8,128)}, u32[]{:S(2)}) copy-start(f32[1,16,4096]{2,1,0:T(8,128)} %param.17) | copy-start | bytes 786436
  15.2 116.5 %copy-start.3 = (s32[1,16]{1,0:T(1,128)S(1)}, s32[1,16]{1,0:T(1,128)}, u32[]{:S(2)}) copy-start(s32[1,16]{1,0:T(1,128)} %param.18) | copy-start | bytes 196
  130.8 106.9 %all-gather.12.cloned.1.call-start = ((), (), s32[]{:S(2)}) async-start(), calls=%async_computation.3 | async-start | bytes 2359296 | tf_op jit(solution)/shard_map/all_gather | solution.py:75
  133.6 163.0 %all-gather.14.cloned.1.call-start = ((), (), s32[]{:S(2)}) async-start(), calls=%async_computation.4 | async-start | bytes 8650752 | tf_op jit(solution)/shard_map/all_gather | solution.py:91
  134.2 246.2 %all-reduce.2.cloned.1.call-start = ((), (), s32[]{:S(2)}) async-start(), calls=%async_computation.5 | async-start | bytes 4194304 | tf_op jit(solution)/shard_map/psum | solution.py:12
Sparse Core Ops, SparseCore 0:
  11.1 44.0 all-gather.7
  57.7 56.4 all-gather.5
  130.9 63.8 all-gather.9
  196.5 41.1 all-gather.11
  240.1 56.4 all-gather.13
  298.8 81.4 all-reduce.1
where the time goes:
time: 405 us
  waiting for transfers between devices  333 us (82%)
  matrix products  44.6 us (11%)
  between operations  16.4 us (4%)
  local copies, waits for them, and re-layouts  6.76 us (2%)
  other arithmetic  4.09 us (1%)
    psum x1, waiting for transfers between devices, from_root(): return lax.psum(kept, axis)  83.7 us
    all_gather x1, waiting for transfers between devices, shards(): y_panel = lax.all_gather(y_tile, 'col', axis=1, tiled=True)  60.4 us
    all_gather x1, waiting for transfers between devices, shards(): lax.all_gather(h_tile, 'col', axis=1, tiled=True)  59.1 us
    all_gather x1, waiting for transfers between devices, shards(): lax.all_gather(s_tile, 'col', axis=1, tiled=True)  49.5 us
    all_gather x1, waiting for transfers between devices, shards(): lax.all_gather(p_tile, 'row', axis=0, tiled=True)  40 us
    all_gather x1, waiting for transfers between devices, shards(): lax.all_gather(s_tile, 'row', axis=0, tiled=True)  39.7 us
    dot_general x1, matrix products, shards(): jnp.dot(lax.all_gather(h_tile, 'col', axis=1, tiled=True), p_columns, pre...  16.5 us
    dot_general x1, matrix products, shards(): lax.dot_general(lax.all_gather(s_tile, 'col', axis=1, tiled=True), y_mirr...  16 us
  transfers between devices with their start and end apart: 6, of which 6 were waited for; matrix products, arithmetic and copies ran while one was open for 4% of the time, Pallas kernels for 0%

commit v1 on v0

--- a/solution.py
+++ b/solution.py
@@ -9,7 +9,12 @@
 
 def from_root(value, axis, source):
     kept = jnp.where(lax.axis_index(axis) == source, value, 0).astype(value.dtype)
-    return lax.psum(kept, axis)
+
+    def panels_remake(base_x):
+        s_next = lax.all_gather(base_x, axis)
+        return jnp.sum(s_next, 0)
+
+    return panels_remake(kept)
 
 
 def assemble(values, places, counts):

time: 405 us -> 496 us (1.22)
  waiting for transfers between devices: 333 us -> 415 us
  other arithmetic: 4.09 us -> 11.5 us
    all_gather x0 -> x1, waiting for transfers between devices: none -> 164 us  [panels_remake(): s_next = lax.all_gather(base_x, axis)]
    psum x1 -> x0, waiting for transfers between devices: 83.7 us -> none  [from_root(): return lax.psum(kept, axis)]
    reduce_sum x0 -> x1, other arithmetic: none -> 7.36 us  [panels_remake(): return jnp.sum(s_next, 0)]
  transfers between devices with their start and end apart: 6 -> 6, of which waited for: 6 -> 6; matrix products, arithmetic and copies ran while one was open for 4% -> 5% of each run, Pallas kernels for 0% -> 0%
where the time goes in v1:
time: 496 us; the launch traced here: 494 us
  waiting for transfers between devices  415 us (84%)
  matrix products  44.1 us (9%)
  between operations  16.4 us (3%)
  other arithmetic  11.5 us (2%)
  local copies, waits for them, and re-layouts  6.74 us (1%)
    all_gather x1, waiting for transfers between devices, panels_remake(): s_next = lax.all_gather(base_x, axis)  164 us
    all_gather x1, waiting for transfers between devices, shards(): y_panel = lax.all_gather(y_tile, 'col', axis=1, tiled=True)  61.2 us
    all_gather x1, waiting for transfers between devices, shards(): lax.all_gather(h_tile, 'col', axis=1, tiled=True)  59.1 us
    all_gather x1, waiting for transfers between devices, shards(): lax.all_gather(s_tile, 'col', axis=1, tiled=True)  51.6 us
    all_gather x1, waiting for transfers between devices, shards(): lax.all_gather(p_tile, 'row', axis=0, tiled=True)  40 us
    all_gather x1, waiting for transfers between devices, shards(): lax.all_gather(s_tile, 'row', axis=0, tiled=True)  39 us
    dot_general x1, matrix products, shards(): jnp.dot(lax.all_gather(h_tile, 'col', axis=1, tiled=True), p_columns, pre...  16.5 us
    dot_general x1, matrix products, shards(): lax.dot_general(lax.all_gather(s_tile, 'col', axis=1, tiled=True), y_mirr...  15.5 us
  transfers between devices with their start and end apart: 6, of which 6 were waited for; matrix products, arithmetic and copies ran while one was open for 5% of the time, Pallas kernels for 0%

profile of v1, /device:TPU:2, one launch (start us, length us, event | category | flops | bytes accessed | tf_op | source)
XLA Modules:
  0.0 494.0 jit_solution(16677526564899280164)
XLA Ops:
  6.5 0.0 all-gather.10.cloned.1.call-start
  7.3 1.1 dot_general.34
  8.4 0.0 copy-start.2
  8.4 1.3 convolution_bitcast_fusion.1
  9.8 0.3 copy.26
  10.0 0.9 reshape.190
  10.9 0.0 all-gather.10.cloned.1.call-update
  10.9 0.0 all-gather.8.cloned.1.call-start
  11.6 0.2 dot_general.31
  11.9 0.7 convolution_bitcast_fusion.2
  12.6 0.3 copy.24
  12.8 0.9 reshape.189
  13.7 0.0 all-gather.8.cloned.1.call-update
  13.7 0.0 all-gather.12.cloned.1.call-start
  14.4 0.0 copy-done.4
  14.4 0.1 convert_reduce_fusion
  14.5 0.1 broadcast_in_dim.19
  14.6 0.2 broadcast_in_dim.20
  14.8 0.3 reshape.188
  15.1 0.0 copy-start.1
  15.2 0.0 copy-start.3
  15.2 40.0 %all-gather.10.cloned.1.call-done = f32[4096,128]{0,1:T(8,128)} async-done(((f32[512,128]{0,1:T(8,128)}), f32[4096,128]{0,1:T(8,128)}) %all-gather.10.cloned.1.call-update) | async-done | bytes 2097168 | tf_op jit(solution)/shard_map/all_gather | solution.py:79
  55.1 59.1 %all-gather.8.cloned.1.call-done = f32[512,4096]{0,1:T(8,128)} async-done(((f32[512,128]{0,1:T(8,128)}), f32[512,4096]{0,1:T(8,128)}) %all-gather.8.cloned.1.call-update) | async-done | bytes 8388624 | tf_op jit(solution)/shard_map/all_gather | solution.py:83
  114.2 16.5 %convolution_multiply_fusion = f32[512,128]{1,0:T(8,128)} fusion(f32[512,128]{1,0:T(8,128)S(1)} %reshape.188, f32[512,4096]{0,1:T(8,128)} %all-gather.8.cloned.1.call-done, f32[4096,128]{0,1:T(8,128)} %all-gather.10.cloned.1.call-done), kind=kOutput, calls=%fused_computation.7 | convolution fusion | flops 3221291008 | bytes 11010048 | tf_op jit(solution)/shard_map/dot_general | solution.py:82
  130.7 0.0 all-gather.12.cloned.1.call-update
  130.8 0.0 all-gather.14.cloned.1.call-start
  131.5 0.0 copy-done.1
  131.5 0.2 dot_general.38
  131.7 0.7 convolution_bitcast_fusion
  132.4 0.3 copy.28
  132.7 0.9 reshape.191
  133.5 0.0 all-gather.14.cloned.1.call-update
  133.5 0.0 all-gather.18.cloned.1.call-start
  133.6 61.2 %all-gather.12.cloned.1.call-done = f32[512,4096]{1,0:T(8,128)} async-done(((f32[512,128]{1,0:T(8,128)}), f32[512,4096]{1,0:T(8,128)}) %all-gather.12.cloned.1.call-update) | async-done | bytes 8388624 | tf_op jit(solution)/shard_map/all_gather | solution.py:88
  194.8 3.2 dynamic-slice_select_fusion
  198.0 0.0 all-gather.18.cloned.1.call-update
  198.0 0.2 all-gather.16.cloned.1.call-start
  198.3 0.3 all-gather.16.cloned.1.call-update
  198.6 39.0 %all-gather.14.cloned.1.call-done = f32[4096,128]{0,1:T(8,128)} async-done(((f32[512,128]{0,1:T(8,128)}), f32[4096,128]{0,1:T(8,128)}) %all-gather.14.cloned.1.call-update) | async-done | bytes 2097168 | tf_op jit(solution)/shard_map/all_gather | solution.py:80
  237.7 9.3 %fusion.29 = f32[512,128]{1,0:T(8,128)S(1)} fusion(f32[512,4096]{1,0:T(8,128)} %all-gather.12.cloned.1.call-done, f32[4096,128]{0,1:T(8,128)} %all-gather.14.cloned.1.call-done), kind=kOutput, calls=%fused_computation.48 | convolution fusion | flops 3221225472 | bytes 10747904 | tf_op jit(solution)/shard_map/dot_general | solution.py:89
  247.0 163.6 %all-gather.18.cloned.1.call-done = f32[1024,4096]{1,0:T(8,128)} async-done(((f32[128,4096]{1,0:T(8,128)}), f32[1024,4096]{1,0:T(8,128)}) %all-gather.18.cloned.1.call-update) | async-done | bytes 16777232 | tf_op jit(solution)/shard_map/all_gather | solution.py:14
  410.7 7.4 %reduce_sum.19 = f32[128,4096]{1,0:T(8,128)S(1)} reduce(f32[8,128,4096]{2,1,0:T(8,128)} %bitcast.88, f32[]{:T(128)} %constant.49.clone.1), dimensions={0}, to_apply=%region_1.2 | reduce | flops 3670016 | bytes 18874372 | tf_op jit(solution)/shard_map/reduce_sum | solution.py:15
  418.0 51.6 %all-gather.16.cloned.1.call-done = f32[512,4096]{0,1:T(8,128)} async-done(((f32[512,128]{0,1:T(8,128)}), f32[512,4096]{0,1:T(8,128)}) %all-gather.16.cloned.1.call-update) | async-done | bytes 8388624 | tf_op jit(solution)/shard_map/all_gather | solution.py:96
  469.6 15.5 %fusion = f32[512,128]{1,0:T(8,128)S(1)} fusion(f32[512,128]{1,0:T(8,128)S(1)} %reshape.188, f32[512,128]{1,0:T(8,128)S(1)} %fusion.29, f32[512,4096]{0,1:T(8,128)} %all-gather.16.cloned.1.call-done, f32[128,4096]{1,0:T(8,128)S(1)} %reduce_sum.19), kind=kOutput, calls=%fused_computation.6 | convolution fusion | flops 3221356544 | bytes 11272192 | tf_op jit(solution)/shard_map/dot_general | solution.py:95
  485.2 0.3 reshape.192
  485.6 0.2 reshape.193
  485.8 0.6 gather_fusion
  486.4 0.8 fusion.7
  (14 shorter events, 0.1 us)
Async XLA Ops:
  6.5 5.1 %copy-start = (f32[1,16,4096]{2,1,0:T(8,128)S(1)}, f32[1,16,4096]{2,1,0:T(8,128)}, u32[]{:S(2)}) copy-start(f32[1,16,4096]{2,1,0:T(8,128)} %param.11) | copy-start | bytes 786436
  6.5 48.6 %all-gather.10.cloned.1.call-start = ((), (), s32[]{:S(2)}) async-start(), calls=%async_computation.1 | async-start | bytes 2359296 | tf_op jit(solution)/shard_map/all_gather | solution.py:79
  8.4 3.5 copy-start.2
  10.9 3.5 copy-start.4
  10.9 103.3 %all-gather.8.cloned.1.call-start = ((), (), s32[]{:S(2)}) async-start(), calls=%async_computation | async-start | bytes 8650752 | tf_op jit(solution)/shard_map/all_gather | solution.py:83
  13.7 181.1 %all-gather.12.cloned.1.call-start = ((), (), s32[]{:S(2)}) async-start(), calls=%async_computation.2 | async-start | bytes 8650752 | tf_op jit(solution)/shard_map/all_gather | solution.py:88
  15.1 116.3 %copy-start.1 = (f32[1,16,4096]{2,1,0:T(8,128)S(1)}, f32[1,16,4096]{2,1,0:T(8,128)}, u32[]{:S(2)}) copy-start(f32[1,16,4096]{2,1,0:T(8,128)} %param.17) | copy-start | bytes 786436
  15.2 116.5 %copy-start.3 = (s32[1,16]{1,0:T(1,128)S(1)}, s32[1,16]{1,0:T(1,128)}, u32[]{:S(2)}) copy-start(s32[1,16]{1,0:T(1,128)} %param.18) | copy-start | bytes 196
  130.8 106.9 %all-gather.14.cloned.1.call-start = ((), (), s32[]{:S(2)}) async-start(), calls=%async_computation.3 | async-start | bytes 2359296 | tf_op jit(solution)/shard_map/all_gather | solution.py:80
  133.5 277.1 %all-gather.18.cloned.1.call-start = ((), (), s32[]{:S(2)}) async-start(), calls=%async_computation.5 | async-start | bytes 18874368 | tf_op jit(solution)/shard_map/all_gather | solution.py:14
  198.0 271.6 %all-gather.16.cloned.1.call-start = ((), (), s32[]{:S(2)}) async-start(), calls=%async_computation.4 | async-start | bytes 8650752 | tf_op jit(solution)/shard_map/all_gather | solution.py:96
Sparse Core Ops, SparseCore 0:
  11.1 44.0 all-gather.9
  57.7 56.4 all-gather.7
  130.9 63.8 all-gather.11
  196.5 41.1 all-gather.13
  239.3 171.3 all-gather.17
  413.1 56.5 all-gather.15
